TPU v7x, 256 devices: a whole 4x4x8 slice. The times are simulated.
256 devices in a mesh: dp: 8 (over z_hi, x), expert: 32 (over z_lo, y, core).
Axes of the slice: x: 4, y: 4, z: 8 (z_hi: 2, z_lo: 4; z = z_hi * 4 + z_lo), core: 2. Of those that a mesh axis runs over, the one named last changes fastest.
Arguments:
- tokens: bfloat16 [32768, 3584], P(('dp', 'expert')), may hold values from -6 to 6
- cotangent: bfloat16 [32768, 3584], P(('dp', 'expert')), may hold values from -0.09375 to 0.09375
- expert_ids: int32 [32768, 8], P(('dp', 'expert')), may hold values from 0 to 255, all different within a row; in each aligned block of 128 rows (0 to 127, 128 to 255, ...) at most 6 rows name the same one
- gates: bfloat16 [32768, 8], P(('dp', 'expert')), may hold values from 0.049804688 to 1
- swap_flags: int32 [16], replicated, may hold values 0 or 1
- gate_w: bfloat16 [32, 3584, 1024], P('expert', None, 'dp'), may hold values from -0.09375 to 0.09375
- up_w: bfloat16 [32, 3584, 1024], P('expert', None, 'dp'), may hold values from -0.09375 to 0.09375
- down_w: bfloat16 [32, 1024, 3584], P('expert', 'dp'), may hold values from -0.1875 to 0.1875
Outputs:
- grad_gate_w: bfloat16 [32, 3584, 1024], P('expert', None, 'dp')
- grad_up_w: bfloat16 [32, 3584, 1024], P('expert', None, 'dp')
- grad_down_w: bfloat16 [32, 1024, 3584], P('expert', 'dp')
- score_grad: float32 [32768, 8], P(('dp', 'expert'))
Inputs may be any that keep to these rules, and one draw needn't show every extreme that they name: `expert_ids`: among the 128 rows of one device no expert is named more than 6 times, a bound that some block reaches; the numbers of one row differ. `swap_flags`: 1 means that slots s and s + 16 trade their experts.
All inputs are finite; a program needn't handle non-finite values.
Results may differ from a plain program's by a relative error of at most 0.011.
Values may be sent and summed in bfloat16 or wider, within the bound.
A program may use at most 128 MiB of HBM per device.

v0:
```python
import jax
import jax.numpy as jnp
from jax import lax
from jax.sharding import PartitionSpec as P

CAP = 6


def partner(block, axis, stride):
    count = lax.axis_size(axis)
    route = []
    for low in range(count):
        high = low | 1 << stride
        if high != low and high < count:
            route += [(low, high), (high, low)]
    return lax.ppermute(block, axis, route)


def body(tokens, cotangent, expert_ids, gates, swap_flags, gate_w, up_w, down_w):
    axis_len = lax.axis_size("expert")
    half_axis = axis_len // 2
    pair_bit = axis_len.bit_length() - 2
    own_slot = lax.axis_index("expert")
    tok_count = tokens.shape[0]
    top_count = expert_ids.shape[1]
    width = tokens.shape[1]
    flat_ids = expert_ids.reshape(-1)
    choice_count = flat_ids.shape[0]
    valid = flat_ids < axis_len
    pair_index = jnp.arange(half_axis, dtype=jnp.int32)
    flag_of = jnp.sum(
        jnp.where((flat_ids % half_axis)[:, None] == pair_index[None, :], swap_flags[None, :], 0),
        axis=1,
    )
    own_flag = jnp.sum(jnp.where(pair_index == own_slot % half_axis, swap_flags, 0))
    target = jnp.where(flag_of == 1, jnp.bitwise_xor(flat_ids, half_axis), flat_ids)
    target = jnp.where(valid, target, 0)
    onehot = jnp.where(
        (target[:, None] == jnp.arange(axis_len, dtype=jnp.int32)[None, :]) & valid[:, None], 1, 0
    ).astype(jnp.int32)
    ranks = jnp.sum(jnp.cumsum(onehot, axis=0) * onehot, axis=1) - 1
    slot_count = axis_len * CAP
    slots = jnp.where(valid, target * CAP + ranks, slot_count)
    source = (
        jnp.full((slot_count,), choice_count, jnp.int32)
        .at[slots]
        .set(jnp.arange(choice_count, dtype=jnp.int32), mode="drop")
    )
    token_index = source // top_count
    padded_x = jnp.concatenate([tokens, jnp.zeros((1, width), tokens.dtype)], axis=0)
    padded_dy = jnp.concatenate([cotangent, jnp.zeros((1, width), cotangent.dtype)], axis=0)
    padded_g = jnp.concatenate([gates.reshape(-1), jnp.zeros((1,), gates.dtype)], axis=0)
    send_x = padded_x[token_index].reshape(axis_len, CAP, width)
    send_dy = padded_dy[token_index].reshape(axis_len, CAP, width)
    send_g = padded_g[source].reshape(axis_len, CAP)
    recv_x, recv_dy, recv_g = (
        lax.all_to_all(send_x, "expert", split_axis=0, concat_axis=0, tiled=True),
        lax.all_to_all(send_dy, "expert", split_axis=0, concat_axis=0, tiled=True),
        lax.all_to_all(send_g, "expert", split_axis=0, concat_axis=0, tiled=True),
    )
    w_gate = gate_w[0]
    w_up = up_w[0]
    w_down = down_w[0]
    other_gate, other_up, other_down = partner((gate_w, up_w, down_w), "expert", pair_bit)
    taken = own_flag == 1
    w_gate = jnp.where(taken, other_gate[0], w_gate)
    w_up = jnp.where(taken, other_up[0], w_up)
    w_down = jnp.where(taken, other_down[0], w_down)
    contract = (((0,), (0,)), ((), ()))
    part_x = lax.all_gather(recv_x, "dp", axis=0, tiled=True)
    part_dy = lax.all_gather(recv_dy, "dp", axis=0, tiled=True)
    part_g = lax.all_gather(recv_g, "dp", axis=0, tiled=True)
    block_count = part_x.shape[0]
    row_x = part_x.reshape(-1, width)
    row_dy = part_dy.reshape(-1, width)
    row_g = part_g.reshape(-1, 1)
    pre_gate = jnp.dot(row_x, w_gate, preferred_element_type=jnp.float32)
    pre_up = jnp.dot(row_x, w_up, preferred_element_type=jnp.float32)
    sigma = jax.nn.sigmoid(pre_gate)
    active = pre_gate * sigma
    hidden = (active * pre_up).astype(jnp.bfloat16)
    back = lax.dot_general(
        row_dy, w_down, (((1,), (1,)), ((), ())), preferred_element_type=jnp.float32
    )
    score = jnp.sum(hidden.astype(jnp.float32) * back, axis=1)
    scaled = row_dy * row_g
    d_hidden = row_g.astype(jnp.float32) * back
    d_gate = (d_hidden * pre_up * sigma * (1.0 + pre_gate * (1.0 - sigma))).astype(jnp.bfloat16)
    d_up = (d_hidden * active).astype(jnp.bfloat16)
    grad_gate = lax.dot_general(row_x, d_gate, contract, preferred_element_type=jnp.float32)
    grad_up = lax.dot_general(row_x, d_up, contract, preferred_element_type=jnp.float32)
    grad_down = lax.dot_general(hidden, scaled, contract, preferred_element_type=jnp.float32)
    scores = score.reshape(block_count, CAP)
    grad_gate, grad_up, grad_down, scores = (grad_gate, grad_up, grad_down, scores)
    summed = lax.psum(scores, "dp")
    own_scores = lax.dynamic_slice_in_dim(summed, lax.axis_index("dp") * axis_len, axis_len, 0)
    returned = lax.all_to_all(own_scores, "expert", split_axis=0, concat_axis=0, tiled=True)
    picked = returned.reshape(-1)[jnp.minimum(slots, slot_count - 1)]
    score_grad = jnp.where(valid, picked, 0.0).reshape(tok_count, top_count)
    out_gate = grad_gate.astype(jnp.bfloat16)[None]
    out_up = grad_up.astype(jnp.bfloat16)[None]
    out_down = grad_down.astype(jnp.bfloat16)[None]
    return (out_gate, out_up, out_down, score_grad)


def solution(mesh):
    placed = (
        P(("dp", "expert"), None),
        P(("dp", "expert"), None),
        P(("dp", "expert"), None),
        P(("dp", "expert"), None),
        P(),
        P("expert", None, "dp"),
        P("expert", None, "dp"),
        P("expert", "dp", None),
    )
    return jax.shard_map(
        body,
        mesh=mesh,
        in_specs=placed,
        out_specs=(
            P("expert", None, "dp"),
            P("expert", None, "dp"),
            P("expert", "dp", None),
            P(("dp", "expert"), None),
        ),
        check_vma=False,
    )
```

profile of v0, /device:TPU:1, one launch (start us, length us, event | category | flops | bytes accessed | tf_op | source)
XLA Modules:
  0.0 742.1 jit_solution(1144176695480367231)
XLA Ops:
  9.1 9.0 %reduce-window.6 = s32[32,8,128]{2,1,0:T(8,128)S(1)} reduce-window(s32[32,8,128]{2,1,0:T(8,128)S(1)} %fusion.31, s32[]{:T(128)} %constant.32.clone.1), window={size=1x1x128 pad=0_0x0_0x127_0}, to_apply=%region_1.2 | reduce-window | flops 4161536 | bytes 262148 | tf_op jit(solution)/shard_map/reduce-window
  18.7 4.3 scatter_custom_fusion
  26.2 54.0 %all_to_all.32 = bf16[32,6,3584]{2,1,0:T(8,128)(2,1)S(1)} all-to-all(bf16[32,6,3584]{2,1,0:T(8,128)(2,1)S(1)} %reshape.224), channel_id=1, replica_groups=mesh['dp'=8,'expert'=32] {'expert'}, dimensions={0} | all-to-all | bytes 2752512 | tf_op jit(solution)/shard_map/all_to_all | solution.py:57
  80.2 1.5 copy.68
  85.0 78.0 %all_to_all.33 = bf16[32,6,3584]{2,1,0:T(8,128)(2,1)S(1)} all-to-all(bf16[32,6,3584]{2,1,0:T(8,128)(2,1)S(1)} %reshape.228), channel_id=1, replica_groups=mesh['dp'=8,'expert'=32] {'expert'}, dimensions={0} | all-to-all | bytes 2752512 | tf_op jit(solution)/shard_map/all_to_all | solution.py:58
  163.0 1.6 copy.72
  168.1 1.6 gather_fusion.1
  170.5 5.8 all-to-all-start.1
  177.6 242.5 %all-to-all-done.1 = bf16[32,1,6]{2,1,0:T(2,128)(2,1)S(1)} async-done(((bf16[32,1,6]{2,1,0:T(2,128)(2,1)}), bf16[32,1,6]{2,1,0:T(2,128)(2,1)S(1)}, u32[]{:S(2)}, u32[]{:S(2)}) %all-to-all-start.1) | async-done | bytes 416 | tf_op jit(solution)/shard_map/all_to_all | solution.py:59
  420.1 43.9 %all-gather = bf16[256,1,6]{2,1,0:T(2,128)(2,1)S(1)} all-gather(bf16[32,1,6]{2,1,0:T(2,128)(2,1)S(1)} %all-to-all-done.1), channel_id=2, replica_groups=mesh['dp'=8,'expert'=32] {'dp'}, dimensions={0}, use_global_device_ids=true | all-gather | bytes 3456 | tf_op jit(solution)/shard_map/all_gather | solution.py:72
  464.5 13.1 %copy.69 = bf16[256,6,3584]{2,1,0:T(8,128)(2,1)} copy(bf16[256,6,3584]{2,0,1:T(8,128)(2,1)} %all-gather.4.cloned.1.call-done) | data formatting | bytes 22020096 | tf_op jit(solution)/shard_map/all_gather | solution.py:70
  477.6 17.7 %reshape.225 = bf16[1536,3584]{1,0:T(8,128)(2,1)} reshape(bf16[256,6,3584]{2,1,0:T(8,128)(2,1)} %copy.69) | data formatting | bytes 22020096 | tf_op jit(solution)/shard_map/reshape | solution.py:74
  495.3 106.1 %all-gather.6.cloned.1.call-done = bf16[256,6,3584]{2,0,1:T(8,128)(2,1)} async-done(((bf16[32,6,3584]{2,0,1:T(8,128)(2,1)}), bf16[256,6,3584]{2,0,1:T(8,128)(2,1)}) %all-gather.6.cloned.1.call-update) | async-done | bytes 11010064 | tf_op jit(solution)/shard_map/all_gather | solution.py:71
  601.5 13.1 %copy.73 = bf16[256,6,3584]{2,1,0:T(8,128)(2,1)} copy(bf16[256,6,3584]{2,0,1:T(8,128)(2,1)} %all-gather.6.cloned.1.call-done) | data formatting | bytes 22020096 | tf_op jit(solution)/shard_map/all_gather | solution.py:71
  614.5 17.8 %reshape.229 = bf16[1536,3584]{1,0:T(8,128)(2,1)} reshape(bf16[256,6,3584]{2,1,0:T(8,128)(2,1)} %copy.73) | data formatting | bytes 22020096 | tf_op jit(solution)/shard_map/reshape | solution.py:75
  632.4 8.0 %fusion.13 = f32[1536,128]{0,1:T(8,128)S(1)} fusion(bf16[1536,3584]{1,0:T(8,128)(2,1)} %reshape.225, bf16[1,3584,128]{2,1,0:T(8,128)(2,1)S(1)} %collective-permute-done.1, bf16[1,3584,128]{2,1,0:T(8,128)(2,1)S(1)} %copy-done, pred[]{:T(512)S(6)} %eq.85), kind=kOutput, calls=%fused_computation.16 | convolution fusion | flops 1409744896 | bytes 13631489 | tf_op jit(solution)/shard_map/dot_general | solution.py:78
  640.4 8.2 %fusion.11 = f32[1536,128]{0,1:T(8,128)S(1)} fusion(bf16[1536,3584]{1,0:T(8,128)(2,1)} %reshape.225, bf16[1,3584,128]{2,1,0:T(8,128)(2,1)} %collective-permute-done.2, bf16[1,3584,128]{2,1,0:T(8,128)(2,1)} %param.13, pred[]{:T(512)S(6)} %eq.85), kind=kOutput, calls=%fused_computation.14 | convolution fusion | flops 1409744896 | bytes 13631489 | tf_op jit(solution)/shard_map/dot_general | solution.py:77
  648.7 5.7 multiply_reduce_fusion
  654.4 4.0 fusion.7
  658.4 4.3 fusion.6
  662.9 41.4 %psum.7 = f32[256,6]{1,0:T(8,128)S(1)} all-reduce(f32[256,6]{1,0:T(8,128)S(1)} %reshape.230), channel_id=1, replica_groups=mesh['dp'=8,'expert'=32] {'dp'}, use_global_device_ids=true, to_apply=%region_7.8 | all-reduce | flops 1536 | bytes 12288 | tf_op jit(solution)/shard_map/psum | solution.py:95
  704.8 14.2 %all-to-all-start.3 = ((f32[32,1,6]{2,1,0:T(1,128)}), f32[32,1,6]{2,1,0:T(1,128)S(1)}, u32[]{:S(2)}, u32[]{:S(2)}) async-start(f32[32,1,6]{2,1,0:T(1,128)} %bitcast.11), calls=%async_computation.3 | async-start | bytes 32768 | tf_op jit(solution)/shard_map/all_to_all | solution.py:97
  719.0 6.9 fusion.8
  727.6 6.8 gather_fusion.3
  (83 shorter events, 17.6 us)
Async XLA Ops:
  7.2 457.4 %all-gather.4.cloned.1.call-start = ((), (), s32[]{:S(2)}) async-start(), calls=%async_computation.4 | async-start | bytes 12386304 | tf_op jit(solution)/shard_map/all_gather | solution.py:70
  81.7 519.7 %all-gather.6.cloned.1.call-start = ((), (), s32[]{:S(2)}) async-start(), calls=%async_computation.5 | async-start | bytes 12386304 | tf_op jit(solution)/shard_map/all_gather | solution.py:71
  83.0 84.8 %copy-start.2 = (bf16[128,8]{0,1:T(8,128)(2,1)S(1)}, bf16[128,8]{0,1:T(8,128)(2,1)}, u32[]{:S(2)}) copy-start(bf16[128,8]{0,1:T(8,128)(2,1)} %param.11) | copy-start | bytes 6148
  83.1 93.3 %copy-start.3 = (s32[16]{0:T(128)S(1)}, s32[16]{0:T(128)}, u32[]{:S(2)}) copy-start(s32[16]{0:T(128)} %param.12) | copy-start | bytes 196
  164.5 467.8 %collective-permute-start.1 = (bf16[1,3584,128]{2,1,0:T(8,128)(2,1)}, bf16[1,3584,128]{2,1,0:T(8,128)(2,1)S(1)}, u32[]{:S(2)}, u32[]{:S(2)}) collective-permute-start(bf16[1,3584,128]{2,1,0:T(8,128)(2,1)} %param.14), channel_id=1, source_target_pairs={{0,16},{16,0},{1,17},{17,1},{2,18},{18,2},{3,19},{19,3},{4,20},{20... | collective-permute-start | bytes 2752520 | tf_op jit(solution)/shard_map/ppermute | solution.py:16
  165.5 474.9 %collective-permute-start.2 = (bf16[1,3584,128]{2,1,0:T(8,128)(2,1)}, bf16[1,3584,128]{2,1,0:T(8,128)(2,1)}, u32[]{:S(2)}, u32[]{:S(2)}) collective-permute-start(bf16[1,3584,128]{2,1,0:T(8,128)(2,1)} %param.13), channel_id=1, source_target_pairs={{0,16},{16,0},{1,17},{17,1},{2,18},{18,2},{3,19},{19,3},{4,20},{20... | collective-permute-start | bytes 2752520 | tf_op jit(solution)/shard_map/ppermute | solution.py:16
  167.0 481.6 %collective-permute-start = (bf16[1,128,3584]{2,1,0:T(8,128)(2,1)}, bf16[1,128,3584]{2,1,0:T(8,128)(2,1)}, u32[]{:S(2)}, u32[]{:S(2)}) collective-permute-start(bf16[1,128,3584]{2,1,0:T(8,128)(2,1)} %param.15), channel_id=1, source_target_pairs={{0,16},{16,0},{1,17},{17,1},{2,18},{18,2},{3,19},{19,3},{4,20},{20... | collective-permute-start | bytes 2752520 | tf_op jit(solution)/shard_map/ppermute | solution.py:16
  170.5 249.6 %all-to-all-start.1 = ((bf16[32,1,6]{2,1,0:T(2,128)(2,1)}), bf16[32,1,6]{2,1,0:T(2,128)(2,1)S(1)}, u32[]{:S(2)}, u32[]{:S(2)}) async-start(bf16[32,1,6]{2,1,0:T(2,128)(2,1)} %all_to_all.27), calls=%async_computation.1 | async-start | bytes 32768 | tf_op jit(solution)/shard_map/all_to_all | solution.py:59
  614.5 17.8 %copy-start = (bf16[1,3584,128]{2,1,0:T(8,128)(2,1)S(1)}, bf16[1,3584,128]{2,1,0:T(8,128)(2,1)}, u32[]{:S(2)}) copy-start(bf16[1,3584,128]{2,1,0:T(8,128)(2,1)} %param.14) | copy-start | bytes 2752516
  632.3 16.3 %slice-start.3 = ((s8[11010048]{0:T(1024)(128)(4,1)}), s8[4194304]{0:T(1024)(128)(4,1)S(1)}, s32[]{:S(2)}) async-start(s8[11010048]{0:T(1024)(128)(4,1)} %bitcast.45), calls=%async_computation.9 | async-start | bytes 8388608
  632.3 16.3 %slice-start.4 = ((s8[11010048]{0:T(1024)(128)(4,1)}), s8[4194304]{0:T(1024)(128)(4,1)S(1)}, s32[]{:S(2)}) async-start(s8[11010048]{0:T(1024)(128)(4,1)} %bitcast.45), calls=%async_computation.10 | async-start | bytes 8388608
  640.4 8.3 %slice-start.5 = ((s8[11010048]{0:T(1024)(128)(4,1)}), s8[2621440]{0:T(1024)(128)(4,1)S(1)}, s32[]{:S(2)}) async-start(s8[11010048]{0:T(1024)(128)(4,1)} %bitcast.45), calls=%async_computation.11 | async-start | bytes 5242880
  640.4 14.0 %slice-start = ((s8[11010048]{0:T(1024)(128)(4,1)}), s8[4194304]{0:T(1024)(128)(4,1)S(1)}, s32[]{:S(2)}) async-start(s8[11010048]{0:T(1024)(128)(4,1)} %bitcast.43), calls=%async_computation.6 | async-start | bytes 8388608
  640.4 14.0 %slice-start.1 = ((s8[11010048]{0:T(1024)(128)(4,1)}), s8[2621440]{0:T(1024)(128)(4,1)S(1)}, s32[]{:S(2)}) async-start(s8[11010048]{0:T(1024)(128)(4,1)} %bitcast.43), calls=%async_computation.7 | async-start | bytes 5242880
  648.6 5.8 slice-start.2
  658.4 60.6 %copy-start.4 = (bf16[1536,128]{0,1:T(8,128)(2,1)S(1)}, bf16[1536,128]{0,1:T(8,128)(2,1)}, u32[]{:S(2)}) copy-start(bf16[1536,128]{0,1:T(8,128)(2,1)} %get-tuple-element.23) | copy-start | bytes 1179652
  662.7 71.9 %copy-start.1 = (s32[128,8]{0,1:T(8,128)S(1)}, s32[128,8]{0,1:T(8,128)}, u32[]{:S(2)}) copy-start(s32[128,8]{0,1:T(8,128)} %param.10) | copy-start | bytes 12292
  704.8 21.5 %all-to-all-start.3 = ((f32[32,1,6]{2,1,0:T(1,128)}), f32[32,1,6]{2,1,0:T(1,128)S(1)}, u32[]{:S(2)}, u32[]{:S(2)}) async-start(f32[32,1,6]{2,1,0:T(1,128)} %bitcast.11), calls=%async_computation.3 | async-start | bytes 32768 | tf_op jit(solution)/shard_map/all_to_all | solution.py:97
Sparse Core Ops, SparseCore 0:
  81.9 288.9 all-gather.3
  373.4 228.0 all-gather.5
where the time goes:
time: 743 us; the launch traced here: 742 us
  waiting for transfers between devices  349 us (47%)
  blocking collectives  217 us (29%)
  local copies, waits for them, and re-layouts  87.8 us (12%)
  matrix products  37.1 us (5%)
  starting transfers between devices  23.4 us (3%)
  between operations  15.1 us (2%)
  other arithmetic  12.4 us (2%)
    all_to_all x1, waiting for transfers between devices, body(): lax.all_to_all(send_g, 'expert', split_axis=0, concat_axis=0, tiled=True)  242 us
    all_gather x1, waiting for transfers between devices, body(): part_dy = lax.all_gather(recv_dy, 'dp', axis=0, tiled=True)  106 us
    all_to_all x1, blocking collectives, body(): lax.all_to_all(send_dy, 'expert', split_axis=0, concat_axis=0, tiled=True)  78 us
    all_to_all x1, blocking collectives, body(): lax.all_to_all(send_x, 'expert', split_axis=0, concat_axis=0, tiled=True)  54 us
    all_gather x1, blocking collectives, body(): part_g = lax.all_gather(recv_g, 'dp', axis=0, tiled=True)  43.9 us
    psum x1, blocking collectives, body(): summed = lax.psum(scores, 'dp')  41.4 us
    reshape x1, local copies, waits for them, and re-layouts, body(): row_dy = part_dy.reshape(-1, width)  17.8 us
    reshape x1, local copies, waits for them, and re-layouts, body(): row_x = part_x.reshape(-1, width)  17.7 us
  transfers between devices with their start and end apart: 7, of which 3 were waited for; matrix products, arithmetic and copies ran while one was open for 12% of the time, Pallas kernels for 0%

commit v1 on v0

--- a/solution.py
+++ b/solution.py
@@ -4,6 +4,7 @@
 from jax.sharding import PartitionSpec as P
 
 CAP = 6
+LANE = 128
 
 
 def partner(block, axis, stride):
@@ -50,14 +51,14 @@
     padded_x = jnp.concatenate([tokens, jnp.zeros((1, width), tokens.dtype)], axis=0)
     padded_dy = jnp.concatenate([cotangent, jnp.zeros((1, width), cotangent.dtype)], axis=0)
     padded_g = jnp.concatenate([gates.reshape(-1), jnp.zeros((1,), gates.dtype)], axis=0)
-    send_x = padded_x[token_index].reshape(axis_len, CAP, width)
-    send_dy = padded_dy[token_index].reshape(axis_len, CAP, width)
-    send_g = padded_g[source].reshape(axis_len, CAP)
-    recv_x, recv_dy, recv_g = (
-        lax.all_to_all(send_x, "expert", split_axis=0, concat_axis=0, tiled=True),
-        lax.all_to_all(send_dy, "expert", split_axis=0, concat_axis=0, tiled=True),
-        lax.all_to_all(send_g, "expert", split_axis=0, concat_axis=0, tiled=True),
+    send_g = padded_g[source]
+    g_cols = jnp.where(
+        jnp.arange(LANE, dtype=jnp.int32)[None, :] == 0, send_g[:, None], jnp.zeros((), gates.dtype)
     )
+    packed = jnp.concatenate([padded_x[token_index], padded_dy[token_index], g_cols], axis=1)
+    row_width = packed.shape[1]
+    packed = packed.reshape(axis_len, CAP, row_width)
+    recv = lax.all_to_all(packed, "expert", split_axis=0, concat_axis=0, tiled=True)
     w_gate = gate_w[0]
     w_up = up_w[0]
     w_down = down_w[0]
@@ -67,13 +68,12 @@
     w_up = jnp.where(taken, other_up[0], w_up)
     w_down = jnp.where(taken, other_down[0], w_down)
     contract = (((0,), (0,)), ((), ()))
-    part_x = lax.all_gather(recv_x, "dp", axis=0, tiled=True)
-    part_dy = lax.all_gather(recv_dy, "dp", axis=0, tiled=True)
-    part_g = lax.all_gather(recv_g, "dp", axis=0, tiled=True)
-    block_count = part_x.shape[0]
-    row_x = part_x.reshape(-1, width)
-    row_dy = part_dy.reshape(-1, width)
-    row_g = part_g.reshape(-1, 1)
+    gathered = lax.all_gather(recv, "dp", axis=0, tiled=True)
+    block_count = lax.axis_size("dp")
+    rows = gathered.reshape(-1, row_width)
+    row_x = rows[:, :width]
+    row_dy = rows[:, width:2 * width]
+    row_g = rows[:, 2 * width:2 * width + 1]
     pre_gate = jnp.dot(row_x, w_gate, preferred_element_type=jnp.float32)
     pre_up = jnp.dot(row_x, w_up, preferred_element_type=jnp.float32)
     sigma = jax.nn.sigmoid(pre_gate)
@@ -90,10 +90,9 @@
     grad_gate = lax.dot_general(row_x, d_gate, contract, preferred_element_type=jnp.float32)
     grad_up = lax.dot_general(row_x, d_up, contract, preferred_element_type=jnp.float32)
     grad_down = lax.dot_general(hidden, scaled, contract, preferred_element_type=jnp.float32)
-    scores = score.reshape(block_count, CAP)
-    grad_gate, grad_up, grad_down, scores = (grad_gate, grad_up, grad_down, scores)
-    summed = lax.psum(scores, "dp")
-    own_scores = lax.dynamic_slice_in_dim(summed, lax.axis_index("dp") * axis_len, axis_len, 0)
+    scores = score.reshape(block_count, axis_len, CAP)
+    own_scores = lax.psum_scatter(scores, "dp", scatter_dimension=0, tiled=True)
+    own_scores = own_scores.reshape(axis_len, CAP)
     returned = lax.all_to_all(own_scores, "expert", split_axis=0, concat_axis=0, tiled=True)
     picked = returned.reshape(-1)[jnp.minimum(slots, slot_count - 1)]
     score_grad = jnp.where(valid, picked, 0.0).reshape(tok_count, top_count)

time: 743 us -> 778 us (1.047)
  waiting for transfers between devices: 349 us -> 521 us
  blocking collectives: 217 us -> 95.2 us
  starting transfers between devices: 23.4 us -> 10.5 us
  local copies, waits for them, and re-layouts: 87.8 us -> 77.6 us
    all_to_all x1 -> x0, waiting for transfers between devices: 242 us -> none  [body(): lax.all_to_all(send_g, 'expert', split_axis=0, concat_axis=0, tiled=True)]
    reduce_scatter x0 -> x1, waiting for transfers between devices: none -> 220 us  [body(): own_scores = lax.psum_scatter(scores, 'dp', scatter_dimension=0, tiled=True)]
    all_gather x2 -> x1, waiting for transfers between devices: 106 us -> 300 us  [body(): gathered = lax.all_gather(recv, 'dp', axis=0, tiled=True)]
    all_gather x1 -> x0, blocking collectives: 43.9 us -> none  [body(): part_g = lax.all_gather(recv_g, 'dp', axis=0, tiled=True)]
    psum x1 -> x0, blocking collectives: 41.4 us -> none  [body(): summed = lax.psum(scores, 'dp')]
    all_to_all x2 -> x1, blocking collectives: 132 us -> 95.2 us  [body(): lax.all_to_all(packed, 'expert', split_axis=0, concat_axis=0, tiled=True)]
    all_gather x2 -> x1, local copies, waits for them, and re-layouts: 26.1 us -> 18.4 us  [body(): gathered = lax.all_gather(recv, 'dp', axis=0, tiled=True)]
    reshape x6 -> x2, local copies, waits for them, and re-layouts: 36.8 us -> 30.6 us  [the longest x1 29.8 us: body(): rows = gathered.reshape(-1, row_width)]
  transfers between devices with their start and end apart: 7 -> 6, of which waited for: 3 -> 3; matrix products, arithmetic and copies ran while one was open for 12% -> 11% of each run, Pallas kernels for 0% -> 0%
where the time goes in v1:
time: 778 us; the launch traced here: 777 us
  waiting for transfers between devices  521 us (67%)
  blocking collectives  95.2 us (12%)
  local copies, waits for them, and re-layouts  77.6 us (10%)
  matrix products  43.1 us (6%)
  between operations  15 us (2%)
  other arithmetic  14 us (2%)
  starting transfers between devices  10.5 us (1%)
    all_gather x1, waiting for transfers between devices, body(): gathered = lax.all_gather(recv, 'dp', axis=0, tiled=True)  300 us
    reduce_scatter x1, waiting for transfers between devices, body(): own_scores = lax.psum_scatter(scores, 'dp', scatter_dimension=0, tiled=True)  220 us
    all_to_all x1, blocking collectives, body(): lax.all_to_all(packed, 'expert', split_axis=0, concat_axis=0, tiled=True)  95.2 us
    reshape x1, local copies, waits for them, and re-layouts, body(): rows = gathered.reshape(-1, row_width)  29.8 us
    all_gather x1, local copies, waits for them, and re-layouts, body(): gathered = lax.all_gather(recv, 'dp', axis=0, tiled=True)  18.4 us
  transfers between devices with their start and end apart: 6, of which 3 were waited for; matrix products, arithmetic and copies ran while one was open for 11% of the time, Pallas kernels for 0%

profile of v1, /device:TPU:1, one launch (start us, length us, event | category | flops | bytes accessed | tf_op | source)
XLA Modules:
  0.0 776.9 jit_solution(12796647943783642334)
XLA Ops:
  9.1 9.0 %reduce-window.6 = s32[32,8,128]{2,1,0:T(8,128)S(1)} reduce-window(s32[32,8,128]{2,1,0:T(8,128)S(1)} %fusion.49, s32[]{:T(128)} %constant.30.clone.1), window={size=1x1x128 pad=0_0x0_0x127_0}, to_apply=%region_1.2 | reduce-window | flops 4161536 | bytes 262148 | tf_op jit(solution)/shard_map/reduce-window
  18.7 4.3 scatter_custom_fusion
  23.1 1.2 concatenate.17
  24.3 1.4 gather_fusion
  26.3 1.2 concatenate.19
  27.5 2.5 gather_fusion.1
  30.0 3.4 concatenate.20
  33.7 1.6 gather_fusion.2
  35.5 1.9 pad_maximum_fusion
  37.5 95.2 %all_to_all.14 = bf16[32,6,7296]{2,1,0:T(8,128)(2,1)S(1)} all-to-all(bf16[32,6,7296]{2,1,0:T(8,128)(2,1)S(1)} %pad_maximum_fusion), channel_id=1, replica_groups=mesh['dp'=8,'expert'=32] {'expert'}, dimensions={0} | all-to-all | bytes 5603328 | tf_op jit(solution)/shard_map/all_to_all | solution.py:61
  132.7 1.9 copy.51
  135.4 1.7 collective-permute-start.2
  139.1 300.3 %all-gather.2.cloned.1.call-done = bf16[256,6,7296]{2,0,1:T(8,128)(2,1)} async-done(((bf16[32,6,7296]{2,0,1:T(8,128)(2,1)}), bf16[256,6,7296]{2,0,1:T(8,128)(2,1)}) %all-gather.2.cloned.1.call-update) | async-done | bytes 22413328 | tf_op jit(solution)/shard_map/all_gather | solution.py:71
  439.4 18.4 %copy.52 = bf16[256,6,7296]{2,1,0:T(8,128)(2,1)} copy(bf16[256,6,7296]{2,0,1:T(8,128)(2,1)} %all-gather.2.cloned.1.call-done) | data formatting | bytes 44826624 | tf_op jit(solution)/shard_map/all_gather | solution.py:71
  457.9 29.8 %reshape.226 = bf16[1536,7296]{1,0:T(8,128)(2,1)} reshape(bf16[256,6,7296]{2,1,0:T(8,128)(2,1)} %copy.52) | data formatting | bytes 44826624 | tf_op jit(solution)/shard_map/reshape | solution.py:73
  488.9 6.8 fusion.11
  495.7 6.9 fusion.9
  502.7 6.6 multiply_reduce_fusion
  510.1 8.2 %fusion.26 = bf16[1,3584,128]{2,1,0:T(8,128)(2,1)} fusion(bf16[1536,7296]{1,0:T(8,128)(2,1)} %reshape.226, f32[1536,128]{0,1:T(8,128)S(1)} %fusion.9, f32[1536,128]{0,1:T(8,128)S(1)} %fusion.11, f32[1536,128]{0,1:T(8,128)S(1)} %get-tuple-element.24, f32[1536]{0:T(1024)S(1)} %mul.69), kind=kOutput, calls=%fused_computation.23 | convolution fusion | flops 1411907584 | bytes 14292992 | tf_op jit(solution)/shard_map/dot_general | solution.py:90
  518.3 8.2 %fusion.23 = bf16[1,3584,128]{2,1,0:T(8,128)(2,1)} fusion(bf16[1536,7296]{1,0:T(8,128)(2,1)} %reshape.226, f32[1536,128]{0,1:T(8,128)S(1)} %get-tuple-element.24, f32[1536]{0:T(1024)S(1)} %mul.69, f32[1536,128]{0,1:T(8,128)S(1)} %fusion.9), kind=kOutput, calls=%fused_computation.22 | convolution fusion | flops 1411121152 | bytes 13506560 | tf_op jit(solution)/shard_map/dot_general | solution.py:91
  526.5 220.1 %reduce-scatter.2.cloned.1.call-done = f32[1,32,6]{2,1,0:T(8,128)} async-done(((f32[8,32,6]{2,1,0:T(8,128)}), f32[1,32,6]{2,1,0:T(8,128)}) %reduce-scatter.2.cloned.1.call-update) | async-done | bytes 784 | tf_op jit(solution)/shard_map/reduce_scatter | solution.py:94
  746.6 7.3 all-to-all-start.1
  753.9 6.4 fusion.29
  762.5 6.8 gather_fusion.3
  (64 shorter events, 10.6 us)
Async XLA Ops:
  7.2 432.3 %all-gather.2.cloned.1.call-start = ((), (), s32[]{:S(2)}) async-start(), calls=%async_computation.3 | async-start | bytes 25214976 | tf_op jit(solution)/shard_map/all_gather | solution.py:71
  25.7 7.7 copy-start.1
  35.5 99.1 %copy-start.3 = (bf16[1,3584,128]{2,1,0:T(8,128)(2,1)S(1)}, bf16[1,3584,128]{2,1,0:T(8,128)(2,1)}, u32[]{:S(2)}) copy-start(bf16[1,3584,128]{2,1,0:T(8,128)(2,1)} %param.14) | copy-start | bytes 2752516
  35.5 102.3 %copy-start.2 = (s32[16]{0:T(128)S(1)}, s32[16]{0:T(128)}, u32[]{:S(2)}) copy-start(s32[16]{0:T(128)} %param.12) | copy-start | bytes 196
  37.5 98.0 %copy-start.4 = (bf16[1,3584,128]{2,1,0:T(8,128)(2,1)S(1)}, bf16[1,3584,128]{2,1,0:T(8,128)(2,1)}, u32[]{:S(2)}) copy-start(bf16[1,3584,128]{2,1,0:T(8,128)(2,1)} %param.13) | copy-start | bytes 2752516
  134.6 612.0 %reduce-scatter.2.cloned.1.call-start = ((), (), s32[]{:S(2)}) async-start(), calls=%async_computation.4 | async-start | bytes 147456 | tf_op jit(solution)/shard_map/reduce_scatter | solution.py:94
  134.6 354.3 %collective-permute-start.1 = (bf16[1,3584,128]{2,1,0:T(8,128)(2,1)S(1)}, bf16[1,3584,128]{2,1,0:T(8,128)(2,1)}, u32[]{:S(2)}, u32[]{:S(2)}) collective-permute-start(bf16[1,3584,128]{2,1,0:T(8,128)(2,1)S(1)} %copy-done.3), channel_id=1, source_target_pairs={{0,16},{16,0},{1,17},{17,1},{2,18},{18,2},{3,19},{19,3},{4,20},{20... | collective-permute-start | bytes 2752520 | tf_op jit(solution)/shard_map/ppermute | solution.py:17
  135.4 360.3 %collective-permute-start.2 = (bf16[1,3584,128]{2,1,0:T(8,128)(2,1)S(1)}, bf16[1,3584,128]{2,1,0:T(8,128)(2,1)}, u32[]{:S(2)}, u32[]{:S(2)}) collective-permute-start(bf16[1,3584,128]{2,1,0:T(8,128)(2,1)S(1)} %copy-done.4), channel_id=1, source_target_pairs={{0,16},{16,0},{1,17},{17,1},{2,18},{18,2},{3,19},{19,3},{4,20},{20... | collective-permute-start | bytes 2752520 | tf_op jit(solution)/shard_map/ppermute | solution.py:17
  137.1 365.6 %collective-permute-start = (bf16[1,128,3584]{2,1,0:T(8,128)(2,1)}, bf16[1,128,3584]{2,1,0:T(8,128)(2,1)}, u32[]{:S(2)}, u32[]{:S(2)}) collective-permute-start(bf16[1,128,3584]{2,1,0:T(8,128)(2,1)} %param.15), channel_id=1, source_target_pairs={{0,16},{16,0},{1,17},{17,1},{2,18},{18,2},{3,19},{19,3},{4,20},{20... | collective-permute-start | bytes 2752520 | tf_op jit(solution)/shard_map/ppermute | solution.py:17
  495.7 6.9 copy-start.5
  746.6 14.6 %all-to-all-start.1 = ((f32[32,1,6]{2,1,0:T(1,128)}), f32[32,1,6]{2,1,0:T(1,128)S(1)}, u32[]{:S(2)}, u32[]{:S(2)}) async-start(f32[32,1,6]{2,1,0:T(1,128)} %bitcast.44), calls=%async_computation.2 | async-start | bytes 32768 | tf_op jit(solution)/shard_map/all_to_all | solution.py:96
  753.9 15.6 %copy-start = (s32[128,8]{0,1:T(8,128)S(1)}, s32[128,8]{0,1:T(8,128)}, u32[]{:S(2)}) copy-start(s32[128,8]{0,1:T(8,128)} %param.10) | copy-start | bytes 12292
Sparse Core Ops, SparseCore 0:
  134.7 304.7 all-gather.1
  510.2 236.3 reduce-scatter.1

commit v2 on v1

--- a/solution.py
+++ b/solution.py
@@ -67,32 +67,32 @@
     w_gate = jnp.where(taken, other_gate[0], w_gate)
     w_up = jnp.where(taken, other_up[0], w_up)
     w_down = jnp.where(taken, other_down[0], w_down)
-    contract = (((0,), (0,)), ((), ()))
     gathered = lax.all_gather(recv, "dp", axis=0, tiled=True)
     block_count = lax.axis_size("dp")
-    rows = gathered.reshape(-1, row_width)
-    row_x = rows[:, :width]
-    row_dy = rows[:, width:2 * width]
-    row_g = rows[:, 2 * width:2 * width + 1]
-    pre_gate = jnp.dot(row_x, w_gate, preferred_element_type=jnp.float32)
-    pre_up = jnp.dot(row_x, w_up, preferred_element_type=jnp.float32)
+    row_x = gathered[:, :, :width]
+    row_dy = gathered[:, :, width:2 * width]
+    row_g = gathered[:, :, 2 * width:2 * width + 1]
+    feature = (((2,), (0,)), ((), ()))
+    rows_contract = (((0, 1), (0, 1)), ((), ()))
+    pre_gate = lax.dot_general(row_x, w_gate, feature, preferred_element_type=jnp.float32)
+    pre_up = lax.dot_general(row_x, w_up, feature, preferred_element_type=jnp.float32)
     sigma = jax.nn.sigmoid(pre_gate)
     active = pre_gate * sigma
     hidden = (active * pre_up).astype(jnp.bfloat16)
     back = lax.dot_general(
-        row_dy, w_down, (((1,), (1,)), ((), ())), preferred_element_type=jnp.float32
+        row_dy, w_down, (((2,), (1,)), ((), ())), preferred_element_type=jnp.float32
     )
-    score = jnp.sum(hidden.astype(jnp.float32) * back, axis=1)
+    score = jnp.sum(hidden.astype(jnp.float32) * back, axis=2)
     scaled = row_dy * row_g
     d_hidden = row_g.astype(jnp.float32) * back
     d_gate = (d_hidden * pre_up * sigma * (1.0 + pre_gate * (1.0 - sigma))).astype(jnp.bfloat16)
     d_up = (d_hidden * active).astype(jnp.bfloat16)
-    grad_gate = lax.dot_general(row_x, d_gate, contract, preferred_element_type=jnp.float32)
-    grad_up = lax.dot_general(row_x, d_up, contract, preferred_element_type=jnp.float32)
-    grad_down = lax.dot_general(hidden, scaled, contract, preferred_element_type=jnp.float32)
-    scores = score.reshape(block_count, axis_len, CAP)
-    own_scores = lax.psum_scatter(scores, "dp", scatter_dimension=0, tiled=True)
-    own_scores = own_scores.reshape(axis_len, CAP)
+    grad_gate = lax.dot_general(row_x, d_gate, rows_contract, preferred_element_type=jnp.float32)
+    grad_up = lax.dot_general(row_x, d_up, rows_contract, preferred_element_type=jnp.float32)
+    grad_down = lax.dot_general(hidden, scaled, rows_contract, preferred_element_type=jnp.float32)
+    scores = score.reshape(block_count, axis_len * CAP)
+    parts = lax.all_to_all(scores, "dp", split_axis=0, concat_axis=0, tiled=True)
+    own_scores = jnp.sum(parts, axis=0).reshape(axis_len, CAP)
     returned = lax.all_to_all(own_scores, "expert", split_axis=0, concat_axis=0, tiled=True)
     picked = returned.reshape(-1)[jnp.minimum(slots, slot_count - 1)]
     score_grad = jnp.where(valid, picked, 0.0).reshape(tok_count, top_count)

time: 778 us -> 676 us (0.87)
  waiting for transfers between devices: 521 us -> 301 us
  starting transfers between devices: 10.5 us -> 174 us
  local copies, waits for them, and re-layouts: 77.6 us -> 30.8 us
    ppermute x3, waiting for transfers between devices: 0.01 us -> 259 us  [partner(): return lax.ppermute(block, axis, route)]
    all_gather x1, waiting for transfers between devices: 300 us -> 41.2 us  [body(): gathered = lax.all_gather(recv, 'dp', axis=0, tiled=True)]
    reduce_scatter x1 -> x0, waiting for transfers between devices: 220 us -> none  [body(): own_scores = lax.psum_scatter(scores, 'dp', scatter_dimension=0, tiled=True)]
    all_to_all x1, starting transfers between devices: 7.28 us -> 168 us  [body(): lax.all_to_all(own_scores, 'expert', split_axis=0, concat_axis=0, tiled=T...]
    reshape x2 -> x0, local copies, waits for them, and re-layouts: 30.6 us -> none  [the longest x1 29.8 us: body(): rows = gathered.reshape(-1, row_width)]
    all_gather x1 -> x0, local copies, waits for them, and re-layouts: 18.4 us -> none  [body(): gathered = lax.all_gather(recv, 'dp', axis=0, tiled=True)]
  transfers between devices with their start and end apart: 6 -> 6, of which waited for: 3 -> 3; matrix products, arithmetic and copies ran while one was open for 11% -> 6% of each run, Pallas kernels for 0% -> 0%
where the time goes in v2:
time: 676 us; the launch traced here: 675 us
  waiting for transfers between devices  301 us (45%)
  starting transfers between devices  174 us (26%)
  blocking collectives  95.2 us (14%)
  matrix products  44.5 us (7%)
  local copies, waits for them, and re-layouts  30.8 us (5%)
  between operations  15 us (2%)
  other arithmetic  14 us (2%)
    ppermute x3, waiting for transfers between devices, partner(): return lax.ppermute(block, axis, route)  259 us
    all_to_all x1, starting transfers between devices, body(): lax.all_to_all(own_scores, 'expert', split_axis=0, concat_axis=0, tiled=T...  168 us
    all_to_all x1, blocking collectives, body(): lax.all_to_all(packed, 'expert', split_axis=0, concat_axis=0, tiled=True)  95.2 us
    all_gather x1, waiting for transfers between devices, body(): gathered = lax.all_gather(recv, 'dp', axis=0, tiled=True)  41.2 us
  transfers between devices with their start and end apart: 6, of which 3 were waited for; matrix products, arithmetic and copies ran while one was open for 6% of the time, Pallas kernels for 0%

profile of v2, /device:TPU:1, one launch (start us, length us, event | category | flops | bytes accessed | tf_op | source)
XLA Modules:
  0.0 675.1 jit_solution(5865024908336281529)
XLA Ops:
  10.0 9.0 %reduce-window.6 = s32[32,8,128]{2,1,0:T(8,128)S(1)} reduce-window(s32[32,8,128]{2,1,0:T(8,128)S(1)} %fusion.58, s32[]{:T(128)} %constant.30.clone.1), window={size=1x1x128 pad=0_0x0_0x127_0}, to_apply=%region_1.2 | reduce-window | flops 4161536 | bytes 262148 | tf_op jit(solution)/shard_map/reduce-window
  19.6 4.3 scatter_custom_fusion
  24.0 1.6 gather_fusion.2
  25.7 1.3 concatenate.19
  27.0 1.4 gather_fusion.1
  28.9 1.2 concatenate.17
  30.2 2.5 gather_fusion
  32.7 3.4 concatenate.18
  36.2 1.9 pad_maximum_fusion
  38.1 95.2 %all_to_all.24 = bf16[32,6,7296]{2,1,0:T(8,128)(2,1)S(1)} all-to-all(bf16[32,6,7296]{2,1,0:T(8,128)(2,1)S(1)} %pad_maximum_fusion), channel_id=1, replica_groups=mesh['dp'=8,'expert'=32] {'expert'}, dimensions={0} | all-to-all | bytes 5603328 | tf_op jit(solution)/shard_map/all_to_all | solution.py:61
  133.3 1.8 copy.80
  136.0 1.6 collective-permute-start.1
  139.7 259.2 %collective-permute-done.2 = bf16[1,3584,128]{2,1,0:T(8,128)(2,1)} collective-permute-done((bf16[1,3584,128]{2,1,0:T(8,128)(2,1)S(1)}, bf16[1,3584,128]{2,1,0:T(8,128)(2,1)}, u32[]{:S(2)}, u32[]{:S(2)}) %collective-permute-start.2) | collective-permute-done | bytes 917536 | tf_op jit(solution)/shard_map/ppermute | solution.py:17
  398.9 41.2 %all-gather.2.cloned.1.call-done = bf16[256,6,7296]{2,0,1:T(8,128)(2,1)} async-done(((bf16[32,6,7296]{2,0,1:T(8,128)(2,1)}), bf16[256,6,7296]{2,0,1:T(8,128)(2,1)}) %all-gather.2.cloned.1.call-update) | async-done | bytes 22413328 | tf_op jit(solution)/shard_map/all_gather | solution.py:70
  440.1 6.4 fusion.9
  446.5 1.2 slice_reduce_fusion
  447.7 6.5 fusion.11
  454.2 8.8 %multiply_reduce_fusion = (f32[256,6]{0,1:T(8,128)S(1)}, bf16[256,6,128]{0,2,1:T(8,128)(2,1)}, f32[256,6,128]{0,2,1:T(8,128)}) fusion(f32[256,6,128]{0,2,1:T(8,128)S(1)} %fusion.11, f32[256,6,128]{0,2,1:T(8,128)S(1)} %fusion.9, bf16[1,128,3584]{2,1,0:T(8,128)(2,1)} %collective-permute-done, bf16[1,128,3584]{2,1,0:T(8,128)(2,1)S(1)} %copy-done.4, ...), kind=kOutput, calls=%fused_computation.38 | convolution fusion | flops 1411512832 | bytes 15603713 | tf_op jit(solution)/shard_map/dot_general | solution.py:82
  463.8 3.3 all-to-all-start.1
  467.2 8.4 %fusion.32 = bf16[1,3584,128]{2,1,0:T(8,128)(2,1)} fusion(bf16[256,6,7296]{2,0,1:T(8,128)(2,1)} %all-gather.2.cloned.1.call-done, f32[256,6,128]{0,2,1:T(8,128)S(1)} %fusion.9, f32[256,6,128]{0,2,1:T(8,128)S(1)} %fusion.11, f32[256,6,128]{0,2,1:T(8,128)} %get-tuple-element.24, f32[256,6]{0,1:T(8,128)S(1)} %mul.69), kind=kOutput, calls=%fused_computation.25 | convolution fusion | flops 1411907584 | bytes 14292992 | tf_op jit(solution)/shard_map/dot_general | solution.py:90
  475.6 8.2 %fusion.35 = bf16[1,3584,128]{2,1,0:T(8,128)(2,1)} fusion(bf16[256,6,7296]{2,0,1:T(8,128)(2,1)} %all-gather.2.cloned.1.call-done, f32[256,6,128]{0,2,1:T(8,128)S(1)} %copy-done.5, f32[256,6]{0,1:T(8,128)S(1)} %mul.69, f32[256,6,128]{0,2,1:T(8,128)S(1)} %fusion.9), kind=kOutput, calls=%fused_computation.26 | convolution fusion | flops 1411121152 | bytes 13506560 | tf_op jit(solution)/shard_map/dot_general | solution.py:91
  484.5 167.5 %all-to-all-start.2 = ((f32[32,1,6]{2,1,0:T(1,128)}), f32[32,1,6]{2,1,0:T(1,128)S(1)}, u32[]{:S(2)}, u32[]{:S(2)}) async-start(f32[32,1,6]{2,1,0:T(1,128)} %bitcast.17), calls=%async_computation.2 | async-start | bytes 32768 | tf_op jit(solution)/shard_map/all_to_all | solution.py:96
  652.1 6.3 fusion.38
  660.7 6.8 %gather_fusion.3 = f32[1024]{0:T(1024)S(1)} fusion(f32[192]{0:T(256)S(1)} %reshape.224, s32[1024]{0:T(1024)S(1)} %broadcast_clamp_fusion), kind=kCustom, calls=%fused_computation.3 | custom fusion | bytes 12288 | tf_op jit(solution)/shard_map/gather | solution.py:97
  (66 shorter events, 10.9 us)
Async XLA Ops:
  7.2 432.9 %all-gather.2.cloned.1.call-start = ((), (), s32[]{:S(2)}) async-start(), calls=%async_computation.3 | async-start | bytes 25214976 | tf_op jit(solution)/shard_map/all_gather | solution.py:70
  36.2 99.0 %copy-start.2 = (bf16[1,3584,128]{2,1,0:T(8,128)(2,1)S(1)}, bf16[1,3584,128]{2,1,0:T(8,128)(2,1)}, u32[]{:S(2)}) copy-start(bf16[1,3584,128]{2,1,0:T(8,128)(2,1)} %param.13) | copy-start | bytes 2752516
  36.2 102.2 %copy-start.1 = (s32[16]{0:T(128)S(1)}, s32[16]{0:T(128)}, u32[]{:S(2)}) copy-start(s32[16]{0:T(128)} %param.12) | copy-start | bytes 196
  38.1 97.9 %copy-start.3 = (bf16[1,3584,128]{2,1,0:T(8,128)(2,1)S(1)}, bf16[1,3584,128]{2,1,0:T(8,128)(2,1)}, u32[]{:S(2)}) copy-start(bf16[1,3584,128]{2,1,0:T(8,128)(2,1)} %param.14) | copy-start | bytes 2752516
  38.1 99.5 %copy-start.4 = (bf16[1,128,3584]{2,1,0:T(8,128)(2,1)S(1)}, bf16[1,128,3584]{2,1,0:T(8,128)(2,1)}, u32[]{:S(2)}) copy-start(bf16[1,128,3584]{2,1,0:T(8,128)(2,1)} %param.15) | copy-start | bytes 2752516
  135.2 263.7 %collective-permute-start.2 = (bf16[1,3584,128]{2,1,0:T(8,128)(2,1)S(1)}, bf16[1,3584,128]{2,1,0:T(8,128)(2,1)}, u32[]{:S(2)}, u32[]{:S(2)}) collective-permute-start(bf16[1,3584,128]{2,1,0:T(8,128)(2,1)S(1)} %copy-done.2), channel_id=1, source_target_pairs={{0,16},{16,0},{1,17},{17,1},{2,18},{18,2},{3,19},{19,3},{4,20},{20... | collective-permute-start | bytes 2752520 | tf_op jit(solution)/shard_map/ppermute | solution.py:17
  136.0 311.7 %collective-permute-start.1 = (bf16[1,3584,128]{2,1,0:T(8,128)(2,1)S(1)}, bf16[1,3584,128]{2,1,0:T(8,128)(2,1)}, u32[]{:S(2)}, u32[]{:S(2)}) collective-permute-start(bf16[1,3584,128]{2,1,0:T(8,128)(2,1)S(1)} %copy-done.3), channel_id=1, source_target_pairs={{0,16},{16,0},{1,17},{17,1},{2,18},{18,2},{3,19},{19,3},{4,20},{20... | collective-permute-start | bytes 2752520 | tf_op jit(solution)/shard_map/ppermute | solution.py:17
  137.7 316.5 %collective-permute-start = (bf16[1,128,3584]{2,1,0:T(8,128)(2,1)S(1)}, bf16[1,128,3584]{2,1,0:T(8,128)(2,1)}, u32[]{:S(2)}, u32[]{:S(2)}) collective-permute-start(bf16[1,128,3584]{2,1,0:T(8,128)(2,1)S(1)} %copy-done.4), channel_id=1, source_target_pairs={{0,16},{16,0},{1,17},{17,1},{2,18},{18,2},{3,19},{19,3},{4,20},{20... | collective-permute-start | bytes 2752520 | tf_op jit(solution)/shard_map/ppermute | solution.py:17
  463.8 19.9 %all-to-all-start.1 = ((f32[8,1,192]{2,1,0:T(1,128)}), f32[8,1,192]{2,1,0:T(1,128)S(1)}, u32[]{:S(2)}, u32[]{:S(2)}) async-start(f32[8,1,192]{2,1,0:T(1,128)} %all_to_all.20), calls=%async_computation.1 | async-start | bytes 16384 | tf_op jit(solution)/shard_map/all_to_all | solution.py:94
  467.2 8.4 %copy-start.5 = (f32[256,6,128]{0,2,1:T(8,128)S(1)}, f32[256,6,128]{0,2,1:T(8,128)}, u32[]{:S(2)}) copy-start(f32[256,6,128]{0,2,1:T(8,128)} %get-tuple-element.24) | copy-start | bytes 2359300
  475.6 176.5 %copy-start.6 = (bf16[256,6,128]{0,2,1:T(8,128)(2,1)S(1)}, bf16[256,6,128]{0,2,1:T(8,128)(2,1)}, u32[]{:S(2)}) copy-start(bf16[256,6,128]{0,2,1:T(8,128)(2,1)} %get-tuple-element.19) | copy-start | bytes 1179652
  484.5 174.8 %all-to-all-start.2 = ((f32[32,1,6]{2,1,0:T(1,128)}), f32[32,1,6]{2,1,0:T(1,128)S(1)}, u32[]{:S(2)}, u32[]{:S(2)}) async-start(f32[32,1,6]{2,1,0:T(1,128)} %bitcast.17), calls=%async_computation.2 | async-start | bytes 32768 | tf_op jit(solution)/shard_map/all_to_all | solution.py:96
  652.1 15.6 %copy-start = (s32[128,8]{0,1:T(8,128)S(1)}, s32[128,8]{0,1:T(8,128)}, u32[]{:S(2)}) copy-start(s32[128,8]{0,1:T(8,128)} %param.10) | copy-start | bytes 12292
Sparse Core Ops, SparseCore 0:
  135.3 304.7 all-gather.1

commit v3 on v2

--- a/solution.py
+++ b/solution.py
@@ -1,6 +1,10 @@
+import functools
+
 import jax
 import jax.numpy as jnp
 from jax import lax
+from jax.experimental import pallas as pl
+from jax.experimental.pallas import tpu as pltpu
 from jax.sharding import PartitionSpec as P
 
 CAP = 6
@@ -15,6 +19,85 @@
         if high != low and high < count:
             route += [(low, high), (high, low)]
     return lax.ppermute(block, axis, route)
+
+
+def dp_gather_kernel(n_dp, ring, x_ref, o_ref, recv, send):
+    me = lax.axis_index("dp")
+    ex = lax.axis_index("expert")
+    rows = x_ref.shape[0]
+    half = rows // 2
+    plane = me // ring
+    pos = me % ring
+    left = plane * ring + (pos + ring - 1) % ring
+    right = plane * ring + (pos + 1) % ring
+    far = plane * ring + (pos + 2) % ring
+    across = (me + ring) % n_dp
+
+    def block(k):
+        return o_ref.at[pl.ds(k * rows, rows)]
+
+    def part(k, i):
+        return o_ref.at[pl.ds(k * rows + i * half, half)]
+
+    def push(src, dst, slot, k, peer):
+        copy = pltpu.make_async_remote_copy(
+            src_ref=src,
+            dst_ref=dst,
+            send_sem=send.at[slot],
+            recv_sem=recv.at[k],
+            device_id=(peer, ex),
+            device_id_type=pl.DeviceIdType.MESH,
+        )
+        copy.start()
+        return copy
+
+    def arrived(k):
+        pltpu.make_async_copy(block(k), block(k), recv.at[k]).wait()
+
+    barrier = pltpu.get_barrier_semaphore()
+    for peer in (left, right, across):
+        pl.semaphore_signal(barrier, inc=1, device_id=(peer, ex), device_id_type=pl.DeviceIdType.MESH)
+    pl.semaphore_wait(barrier, 3)
+
+    local = pltpu.make_async_copy(x_ref, block(me), recv.at[me])
+    local.start()
+    sent = [
+        push(x_ref, block(me), 0, me, across),
+        push(x_ref, block(me), 1, me, left),
+        push(x_ref, block(me), 2, me, right),
+    ]
+    arrived(left)
+    sent.append(push(part(left, 0), part(left, 0), 3, left, right))
+    arrived(right)
+    sent.append(push(part(right, 1), part(right, 1), 4, right, left))
+    arrived(across)
+    sent.append(push(block(across), block(across), 5, across, left))
+    sent.append(push(block(across), block(across), 6, across, right))
+    left_across = (left + ring) % n_dp
+    right_across = (right + ring) % n_dp
+    arrived(left_across)
+    sent.append(push(part(left_across, 0), part(left_across, 0), 7, left_across, right))
+    arrived(right_across)
+    sent.append(push(part(right_across, 1), part(right_across, 1), 8, right_across, left))
+    arrived(far)
+    arrived((far + ring) % n_dp)
+    local.wait()
+    for copy in sent:
+        copy.wait_send()
+
+
+def dp_gather(block):
+    n_dp = lax.axis_size("dp")
+    ring = n_dp // 2
+    rows = block.shape[0]
+    return pl.pallas_call(
+        functools.partial(dp_gather_kernel, n_dp, ring),
+        out_shape=jax.ShapeDtypeStruct((n_dp * rows,) + block.shape[1:], block.dtype),
+        in_specs=[pl.BlockSpec(memory_space=pl.ANY)],
+        out_specs=pl.BlockSpec(memory_space=pl.ANY),
+        scratch_shapes=[pltpu.SemaphoreType.DMA((n_dp,)), pltpu.SemaphoreType.DMA((9,))],
+        compiler_params=pltpu.CompilerParams(collective_id=0, has_side_effects=True),
+    )(block)
 
 
 def body(tokens, cotangent, expert_ids, gates, swap_flags, gate_w, up_w, down_w):
@@ -67,7 +150,7 @@
     w_gate = jnp.where(taken, other_gate[0], w_gate)
     w_up = jnp.where(taken, other_up[0], w_up)
     w_down = jnp.where(taken, other_down[0], w_down)
-    gathered = lax.all_gather(recv, "dp", axis=0, tiled=True)
+    gathered = dp_gather(recv)
     block_count = lax.axis_size("dp")
     row_x = gathered[:, :, :width]
     row_dy = gathered[:, :, width:2 * width]

time: 676 us -> 653 us (0.966)
  Pallas kernels: 0 us -> 246 us
  waiting for transfers between devices: 301 us -> 136 us
  blocking collectives: 95.2 us -> 0 us
  starting transfers between devices: 174 us -> 128 us
  other arithmetic: 14 us -> 40.1 us
  local copies, waits for them, and re-layouts: 30.8 us -> 54 us
  between operations: 15 us -> 1.64 us
    ppermute x3, waiting for transfers between devices: 259 us -> 0.01 us  [partner(): return lax.ppermute(block, axis, route)]
    pallas_call x0 -> x1, Pallas kernels: none -> 246 us  [dp_gather(): pl.pallas_call(functools.partial(dp_gather_kernel, n_dp, ring), out_shape...]
    all_to_all x0 -> x1, waiting for transfers between devices: none -> 136 us  [body(): lax.all_to_all(packed, 'expert', split_axis=0, concat_axis=0, tiled=True)]
    all_to_all x1 -> x0, blocking collectives: 95.2 us -> none  [body(): lax.all_to_all(packed, 'expert', split_axis=0, concat_axis=0, tiled=True)]
    all_to_all x1, starting transfers between devices: 168 us -> 109 us  [body(): lax.all_to_all(own_scores, 'expert', split_axis=0, concat_axis=0, tiled=T...]
    all_gather x1 -> x0, waiting for transfers between devices: 41.2 us -> none  [body(): gathered = lax.all_gather(recv, 'dp', axis=0, tiled=True)]
    mul x0 -> x1, other arithmetic: none -> 24.6 us  [body(): scaled = row_dy * row_g]
    slice x2 -> x3, local copies, waits for them, and re-layouts: 0.22 us -> 18.9 us  [the longest x1 18.7 us: body(): row_x = gathered[:, :, :width]]
  transfers between devices with their start and end apart: 6 -> 6, of which waited for: 3 -> 1; matrix products, arithmetic and copies ran while one was open for 6% -> 13% of each run, Pallas kernels for 0% -> 38%
where the time goes in v3:
time: 653 us; the launch traced here: 651 us
  Pallas kernels  246 us (38%)
  waiting for transfers between devices  136 us (21%)
  starting transfers between devices  128 us (20%)
  local copies, waits for them, and re-layouts  54 us (8%)
  matrix products  45.5 us (7%)
  other arithmetic  40.1 us (6%)
    pallas_call x1, Pallas kernels, dp_gather(): pl.pallas_call(functools.partial(dp_gather_kernel, n_dp, ring), out_shape...  246 us
    all_to_all x1, waiting for transfers between devices, body(): lax.all_to_all(packed, 'expert', split_axis=0, concat_axis=0, tiled=True)  136 us
    all_to_all x1, starting transfers between devices, body(): lax.all_to_all(own_scores, 'expert', split_axis=0, concat_axis=0, tiled=T...  109 us
    mul x1, other arithmetic, body(): scaled = row_dy * row_g  24.6 us
    slice x1, local copies, waits for them, and re-layouts, body(): row_x = gathered[:, :, :width]  18.7 us
  transfers between devices with their start and end apart: 6, of which 1 were waited for; matrix products, arithmetic and copies ran while one was open for 13% of the time, Pallas kernels for 38%

profile of v3, /device:TPU:1, one launch (start us, length us, event | category | flops | bytes accessed | tf_op | source)
XLA Modules:
  0.0 651.4 jit_solution(4290842413253174677)
XLA Ops:
  2.6 9.0 %reduce-window.6 = s32[32,8,128]{2,1,0:T(8,128)S(1)} reduce-window(s32[32,8,128]{2,1,0:T(8,128)S(1)} %fusion.36, s32[]{:T(128)} %constant.30.clone.1), window={size=1x1x128 pad=0_0x0_0x127_0}, to_apply=%region_1.2 | reduce-window | flops 4161536 | bytes 262148 | tf_op jit(solution)/shard_map/reduce-window
  12.1 4.3 scatter_custom_fusion
  17.7 2.5 gather_fusion
  20.3 2.4 concatenate.18
  23.9 2.5 gather_fusion.1
  26.4 3.4 concatenate.20
  31.9 3.3 pad_maximum_fusion
  35.2 10.2 %all-to-all-start = ((bf16[32,6,7296]{2,1,0:T(8,128)(2,1)}), bf16[32,6,7296]{2,1,0:T(8,128)(2,1)}, u32[]{:S(2)}, u32[]{:S(2)}) async-start(bf16[32,6,7296]{2,1,0:T(8,128)(2,1)} %pad_maximum_fusion), calls=%async_computation | async-start | bytes 7471104 | tf_op jit(solution)/shard_map/all_to_all | solution.py:144
  45.4 2.4 collective-permute-start.1
  47.9 2.3 collective-permute-start
  51.5 136.3 %all-to-all-done.x_ref = bf16[32,6,7296]{2,1,0:T(8,128)(2,1)} async-done(((bf16[32,6,7296]{2,1,0:T(8,128)(2,1)}), bf16[32,6,7296]{2,1,0:T(8,128)(2,1)}, u32[]{:S(2)}, u32[]{:S(2)}) %all-to-all-start) | async-done | bytes 2801696 | tf_op jit(solution)/shard_map/all_to_all | solution.py:144
  187.8 245.8 %shard_map.111 = bf16[256,6,7296]{2,1,0:T(8,128)(2,1)} custom-call(bf16[32,6,7296]{2,1,0:T(8,128)(2,1)} %all-to-all-done.x_ref), custom_call_target="tpu_custom_call" | custom-call | tf_op jit(solution)/shard_map/pallas_call | solution.py:93
  434.7 1.6 copy.120
  436.3 24.6 %broadcast_multiply_fusion = (bf16[256,6,3584]{2,1,0:T(8,128)(2,1)}, bf16[256,6,3584]{2,1,0:T(8,128)(2,1)}, bf16[256,6,3584]{2,1,0:T(8,128)(2,1)}) fusion(bf16[256,6]{1,0:T(8,128)(2,1)S(1)} %bitcast.71, bf16[256,6,7296]{2,1,0:T(8,128)(2,1)} %shard_map.111), kind=kLoop, calls=%fused_computation.9 | loop fusion | flops 5505024 | bytes 55053312 | tf_op jit(solution)/shard_map/mul | solution.py:169
  461.3 18.7 %copy.104 = bf16[256,6,3584]{0,2,1:T(8,128)(2,1)} copy(bf16[256,6,3584]{2,1,0:T(8,128)(2,1)} %get-tuple-element.24) | data formatting | bytes 22020096 | tf_op jit(solution)/shard_map/slice | solution.py:155
  480.0 6.2 fusion.19
  487.5 3.8 fusion.17
  492.2 6.2 multiply_reduce_fusion
  499.2 4.1 all-to-all-start.1
  503.3 8.3 %fusion.16 = bf16[1,3584,128]{2,1,0:T(8,128)(2,1)} fusion(bf16[256,6,3584]{0,2,1:T(8,128)(2,1)} %copy.104, f32[256,6,128]{0,2,1:T(8,128)} %copy-done.4, f32[256,6,128]{0,2,1:T(8,128)S(1)} %fusion.19, f32[256,6,128]{0,2,1:T(8,128)S(1)} %get-tuple-element.27, f32[256,6]{0,1:T(8,128)S(1)} %bitcast_convert_fusion), kind=kOutput, calls=%fused_computation.18 | convolution fusion | flops 1411907584 | bytes 14292992 | tf_op jit(solution)/shard_map/dot_general | solution.py:173
  511.7 8.2 %fusion.15 = bf16[1,3584,128]{2,1,0:T(8,128)(2,1)} fusion(bf16[256,6,3584]{0,2,1:T(8,128)(2,1)} %copy.104, f32[256,6,128]{0,2,1:T(8,128)S(1)} %get-tuple-element.27, f32[256,6]{0,1:T(8,128)S(1)} %bitcast_convert_fusion, f32[256,6,128]{0,2,1:T(8,128)S(1)} %copy-done.5), kind=kOutput, calls=%fused_computation.17 | convolution fusion | flops 1411121152 | bytes 13506560 | tf_op jit(solution)/shard_map/dot_general | solution.py:174
  520.6 109.1 %all-to-all-start.2 = ((f32[32,1,6]{2,1,0:T(1,128)}), f32[32,1,6]{2,1,0:T(1,128)S(1)}, u32[]{:S(2)}, u32[]{:S(2)}) async-start(f32[32,1,6]{2,1,0:T(1,128)} %bitcast.19), calls=%async_computation.2 | async-start | bytes 32768 | tf_op jit(solution)/shard_map/all_to_all | solution.py:179
  629.7 12.8 %fusion.12 = bf16[1,128,3584]{2,1,0:T(8,128)(2,1)} fusion(bf16[256,6,128]{0,2,1:T(8,128)(2,1)S(1)} %copy-done.6, bf16[256,6,3584]{2,1,0:T(8,128)(2,1)} %get-tuple-element.22), kind=kOutput, calls=%fused_computation.16 | convolution fusion | flops 1409744896 | bytes 12320768 | tf_op jit(solution)/shard_map/dot_general | solution.py:175
  643.8 6.8 %gather_fusion.3 = f32[1024]{0:T(1024)S(1)} fusion(f32[192]{0:T(256)S(1)} %reshape.224, s32[1024]{0:T(1024)S(1)} %broadcast_clamp_fusion), kind=kCustom, calls=%fused_computation.3 | custom fusion | bytes 12288 | tf_op jit(solution)/shard_map/gather | solution.py:180
  (77 shorter events, 15.0 us)
Async XLA Ops:
  20.3 9.5 %copy-start.2 = (bf16[128,8]{0,1:T(8,128)(2,1)S(1)}, bf16[128,8]{0,1:T(8,128)(2,1)}, u32[]{:S(2)}) copy-start(bf16[128,8]{0,1:T(8,128)(2,1)} %param.11) | copy-start | bytes 6148
  26.4 23.8 %copy-start.3 = (s32[16]{0:T(128)S(1)}, s32[16]{0:T(128)}, u32[]{:S(2)}) copy-start(s32[16]{0:T(128)} %param.12) | copy-start | bytes 196
  35.2 152.6 %all-to-all-start = ((bf16[32,6,7296]{2,1,0:T(8,128)(2,1)}), bf16[32,6,7296]{2,1,0:T(8,128)(2,1)}, u32[]{:S(2)}, u32[]{:S(2)}) async-start(bf16[32,6,7296]{2,1,0:T(8,128)(2,1)} %pad_maximum_fusion), calls=%async_computation | async-start | bytes 7471104 | tf_op jit(solution)/shard_map/all_to_all | solution.py:144
  45.4 434.6 %collective-permute-start.1 = (bf16[1,3584,128]{2,1,0:T(8,128)(2,1)}, bf16[1,3584,128]{2,1,0:T(8,128)(2,1)}, u32[]{:S(2)}, u32[]{:S(2)}) collective-permute-start(bf16[1,3584,128]{2,1,0:T(8,128)(2,1)} %param.14), channel_id=1, source_target_pairs={{0,16},{16,0},{1,17},{17,1},{2,18},{18,2},{3,19},{19,3},{4,20},{20... | collective-permute-start | bytes 2752520 | tf_op jit(solution)/shard_map/ppermute | solution.py:21
  47.8 438.4 %collective-permute-start.2 = (bf16[1,3584,128]{2,1,0:T(8,128)(2,1)}, bf16[1,3584,128]{2,1,0:T(8,128)(2,1)S(1)}, u32[]{:S(2)}, u32[]{:S(2)}) collective-permute-start(bf16[1,3584,128]{2,1,0:T(8,128)(2,1)} %param.13), channel_id=1, source_target_pairs={{0,16},{16,0},{1,17},{17,1},{2,18},{18,2},{3,19},{19,3},{4,20},{20... | collective-permute-start | bytes 2752520 | tf_op jit(solution)/shard_map/ppermute | solution.py:21
  47.9 443.4 %collective-permute-start = (bf16[1,128,3584]{2,1,0:T(8,128)(2,1)}, bf16[1,128,3584]{2,1,0:T(8,128)(2,1)S(1)}, u32[]{:S(2)}, u32[]{:S(2)}) collective-permute-start(bf16[1,128,3584]{2,1,0:T(8,128)(2,1)} %param.15), channel_id=1, source_target_pairs={{0,16},{16,0},{1,17},{17,1},{2,18},{18,2},{3,19},{19,3},{4,20},{20... | collective-permute-start | bytes 2752520 | tf_op jit(solution)/shard_map/ppermute | solution.py:21
  480.0 7.5 %copy-start = (bf16[256,6,3584]{0,2,1:T(8,128)(2,1)S(1)}, bf16[256,6,3584]{0,2,1:T(8,128)(2,1)}, u32[]{:S(2)}) copy-start(bf16[256,6,3584]{0,2,1:T(8,128)(2,1)} %copy.104) | copy-start | bytes 33030148
  480.0 11.3 %slice-start = ((s8[14680064]{0:T(1024)(128)(4,1)}), s8[4194304]{0:T(1024)(128)(4,1)S(1)}, s32[]{:S(2)}) async-start(s8[14680064]{0:T(1024)(128)(4,1)} %bitcast.68), calls=%async_computation.3 | async-start | bytes 8388608
  480.0 11.3 %slice-start.1 = ((s8[14680064]{0:T(1024)(128)(4,1)}), s8[4194304]{0:T(1024)(128)(4,1)S(1)}, s32[]{:S(2)}) async-start(s8[14680064]{0:T(1024)(128)(4,1)} %bitcast.68), calls=%async_computation.4 | async-start | bytes 8388608
  486.2 5.4 slice-start.2
  486.2 6.0 slice-start.3
  491.3 7.1 %copy-start.4 = (f32[256,6,128]{0,2,1:T(8,128)}, f32[256,6,128]{0,2,1:T(8,128)S(1)}, u32[]{:S(2)}) copy-start(f32[256,6,128]{0,2,1:T(8,128)S(1)} %fusion.17) | copy-start | bytes 2359300
  498.4 13.3 %copy-start.5 = (f32[256,6,128]{0,2,1:T(8,128)S(1)}, f32[256,6,128]{0,2,1:T(8,128)}, u32[]{:S(2)}) copy-start(f32[256,6,128]{0,2,1:T(8,128)} %copy-done.4) | copy-start | bytes 2359300
  499.2 20.6 %all-to-all-start.1 = ((f32[8,1,192]{2,1,0:T(1,128)}), f32[8,1,192]{2,1,0:T(1,128)S(1)}, u32[]{:S(2)}, u32[]{:S(2)}) async-start(f32[8,1,192]{2,1,0:T(1,128)} %all_to_all.20), calls=%async_computation.1 | async-start | bytes 16384 | tf_op jit(solution)/shard_map/all_to_all | solution.py:177
  511.7 118.0 %copy-start.6 = (bf16[256,6,128]{0,2,1:T(8,128)(2,1)S(1)}, bf16[256,6,128]{0,2,1:T(8,128)(2,1)}, u32[]{:S(2)}) copy-start(bf16[256,6,128]{0,2,1:T(8,128)(2,1)} %get-tuple-element.19) | copy-start | bytes 1179652
  519.8 131.0 %copy-start.1 = (s32[128,8]{0,1:T(8,128)S(1)}, s32[128,8]{0,1:T(8,128)}, u32[]{:S(2)}) copy-start(s32[128,8]{0,1:T(8,128)} %param.10) | copy-start | bytes 12292
  520.6 121.9 %all-to-all-start.2 = ((f32[32,1,6]{2,1,0:T(1,128)}), f32[32,1,6]{2,1,0:T(1,128)S(1)}, u32[]{:S(2)}, u32[]{:S(2)}) async-start(f32[32,1,6]{2,1,0:T(1,128)} %bitcast.19), calls=%async_computation.2 | async-start | bytes 32768 | tf_op jit(solution)/shard_map/all_to_all | solution.py:179
